TPU v7x, 32 devices: a whole 2x2x4 slice. The times are simulated.
32 devices in a mesh: xy: 8 (over y, x, core), gz: 4 (over z).
Axes of the slice: x: 2, y: 2, z: 4, core: 2. Of those that a mesh axis runs over, the one named last changes fastest.
Arguments:
- features: bfloat16 [8, 2, 4, 64, 128], P('xy', None, 'gz'), may hold values from -6 to 6
- cotangent: bfloat16 [8, 2, 4, 64, 128], P('xy', None, 'gz'), may hold values from -6 to 6
- positions: float32 [8, 2, 4, 3, 64], P('xy', None, 'gz'), may hold values from 0 to 1
- counts: int32 [8, 2, 4], P('xy', None, 'gz'), may hold values from 32 to 64
- neighbour_mask: int32 [8, 2, 4, 27], P('xy', None, 'gz'), may hold values 0 or 1
- proj_weight: bfloat16 [128, 64], replicated, may hold values from -0.5 to 0.5
- out_weight: bfloat16 [64, 128], replicated, may hold values from -0.75 to 0.75
- radial_weight: float32 [8, 64], replicated, may hold values from -58 to 58
Outputs:
- updated: bfloat16 [8, 2, 4, 64, 128], P('xy', None, 'gz')
- feature_grad: bfloat16 [8, 2, 4, 64, 128], P('xy', None, 'gz')
Inputs may be any that keep to these rules, and one draw needn't show every extreme that they name: `counts`: the atoms of a cell beyond its count are padding.
All inputs are finite; a program needn't handle non-finite values. No bound on the sum of `neighbour_mask` on one device may be relied on, other than what follows from the above.
Results may differ from a plain program's by a relative error of at most 0.007.
Values may be sent and summed in bfloat16 or wider, within the bound.
A program may use at most 64 MiB of HBM per device.

v0:
```python
import jax
import jax.numpy as jnp
from jax import lax
from jax.sharding import PartitionSpec as P

BASES = 8


def shifted(block, axis, distance):
    devices = range(lax.axis_size(axis))
    route = [((i - distance) % len(devices), i) for i in devices]
    return lax.ppermute(block, axis, route)


def with_halo(x, sides, width):
    for axis, dim in sides:
        peers, length = (lax.axis_size(axis), x.shape[dim])
        up = [(i, (i + 1) % peers) for i in range(peers)]
        down = [(j, i) for i, j in up]
        last = lax.slice_in_dim(x, length - width, length, axis=dim)
        initial = lax.slice_in_dim(x, 0, width, axis=dim)
        before = lax.ppermute(last, axis, up)
        after = lax.ppermute(initial, axis, down)
        x = jnp.concatenate([before, x, after], axis=dim)
    return x


def build_tiles(own_pos, own_valid, other_pos, other_valid, cell_gate, shift_vec, self_flag):
    separation = other_pos[:, :, None, :] + shift_vec[None, :, None, None] - own_pos[:, :, :, None]
    squared = 4.0 * jnp.sum(separation * separation, axis=1)
    atom_count = own_pos.shape[2]
    diagonal_ones = (jnp.arange(atom_count)[:, None] == jnp.arange(atom_count)[None, :]).astype(
        jnp.float32
    )
    pair_keep = own_valid[:, :, None] * other_valid[:, None, :] * cell_gate[:, None, None]
    pair_keep = pair_keep * (1.0 - self_flag * diagonal_ones)
    envelope = jnp.square(jnp.maximum(1.0 - squared, 0.0)) * pair_keep
    basis_list = [
        (envelope * jnp.exp(-2.0 * jnp.square(BASES * squared - which_basis - 0.5))).astype(
            jnp.bfloat16
        )
        for which_basis in range(BASES)
    ]
    return jnp.stack(basis_list, axis=1)


def direction_shifts(direction):
    return (direction // 9 - 1, direction // 3 % 3 - 1, direction % 3 - 1)


def neighbour_of(padded, shift_x, shift_y, shift_z):
    layer_slab = lax.dynamic_index_in_dim(padded, shift_x + 1, 0, keepdims=False)
    layer_slab = lax.dynamic_index_in_dim(layer_slab, shift_z + 1, 1, keepdims=False)
    return jnp.roll(layer_slab, -shift_y, axis=0)


def all_tiles(geom_halo, own_geom):

    def one_direction(direction):
        shift_x, shift_y, shift_z = direction_shifts(direction)
        other_geom = neighbour_of(geom_halo, shift_x, shift_y, shift_z)
        own_listed = lax.dynamic_index_in_dim(own_geom[:, 4], direction, 1, keepdims=False)
        other_listed = lax.dynamic_index_in_dim(other_geom[:, 4], 26 - direction, 1, keepdims=False)
        shift_vec = jnp.stack([shift_x, shift_y, shift_z]).astype(jnp.float32)
        self_flag = (direction == 13).astype(jnp.float32)
        return build_tiles(
            own_geom[:, :3],
            own_geom[:, 3],
            other_geom[:, :3],
            other_geom[:, 3],
            own_listed * other_listed,
            shift_vec,
            self_flag,
        )

    return lax.map(one_direction, jnp.arange(27, dtype=jnp.int32))


def gather_messages(source_halo, tile_stack, radial_weight):

    def add_pair(direction, running):
        shift_x, shift_y, shift_z = direction_shifts(direction)
        tile_set = lax.dynamic_index_in_dim(tile_stack, direction, 0, keepdims=False)
        other_source = neighbour_of(source_halo, shift_x, shift_y, shift_z)
        per_basis = jnp.einsum(
            "cbij,ckj->cbki", tile_set, other_source, preferred_element_type=jnp.float32
        )
        return running + jnp.einsum(
            "cbki,bk->cki", per_basis, radial_weight, precision=lax.Precision.HIGHEST
        )

    empty_sum = jnp.zeros(
        (tile_stack.shape[1], source_halo.shape[3], source_halo.shape[4]), jnp.float32
    )
    return lax.fori_loop(0, 27, add_pair, empty_sum)


def return_partials(grad_msg, tile_stack, radial_weight):
    cell_count, channel_count, atom_count = grad_msg.shape

    def add_back(direction, returned):
        shift_x, shift_y, shift_z = direction_shifts(direction)
        tile_set = lax.dynamic_index_in_dim(tile_stack, direction, 0, keepdims=False)
        per_basis = jnp.einsum(
            "cbij,cki->cbkj", tile_set, grad_msg, preferred_element_type=jnp.float32
        )
        partial_sum = jnp.einsum(
            "cbkj,bk->ckj", per_basis, radial_weight, precision=lax.Precision.HIGHEST
        )
        partial_sum = jnp.roll(partial_sum, shift_y, axis=0)
        corner = (shift_x + 1, 0, shift_z + 1, 0, 0)
        current = lax.dynamic_slice(returned, corner, (1, cell_count, 1, channel_count, atom_count))
        return lax.dynamic_update_slice(returned, current + partial_sum[None, :, None], corner)

    returned = lax.fori_loop(
        0, 27, add_back, jnp.zeros((3, cell_count, 3, channel_count, atom_count), jnp.float32)
    )
    from_below = shifted(returned[:, :, 2].astype(jnp.bfloat16), "gz", 1).astype(jnp.float32)
    from_above = shifted(returned[:, :, 0].astype(jnp.bfloat16), "gz", -1).astype(jnp.float32)
    folded = returned[:, :, 1] + from_below + from_above
    from_left = shifted(folded[2].astype(jnp.bfloat16), "xy", 1).astype(jnp.float32)
    from_right = shifted(folded[0].astype(jnp.bfloat16), "xy", -1).astype(jnp.float32)
    return folded[1] + from_left + from_right


def on_device(
    features, cotangent, positions, counts, neighbour_mask, proj_weight, out_weight, radial_weight
):
    atom_count = features.shape[3]
    inputs = features[0, :, 0]
    cot_cells = cotangent[0, :, 0]
    valid_atom = (
        jnp.arange(atom_count, dtype=jnp.int32)[None, None, None, :] < counts[..., None]
    ).astype(jnp.float32)
    mask_float = neighbour_mask.astype(jnp.float32)
    listed_row = jnp.pad(
        mask_float, ((0, 0), (0, 0), (0, 0), (0, atom_count - mask_float.shape[3]))
    )
    geometry = jnp.concatenate(
        [positions, valid_atom[:, :, :, None], listed_row[:, :, :, None]], axis=3
    )
    projected = jnp.einsum(
        "cin,nk->cki", inputs, proj_weight, preferred_element_type=jnp.float32
    ).astype(jnp.bfloat16)
    geom_halo = with_halo(geometry, (("xy", 0), ("gz", 2)), 1)
    proj_halo = with_halo(projected[None, :, None], (("xy", 0), ("gz", 2)), 1)
    own_geom = geometry[0, :, 0]
    tile_stack = all_tiles(geom_halo, own_geom)
    message = gather_messages(proj_halo, tile_stack, radial_weight)
    activated = jax.nn.silu(message).astype(jnp.bfloat16)
    updated = (
        inputs.astype(jnp.float32)
        + jnp.einsum("cki,kn->cin", activated, out_weight, preferred_element_type=jnp.float32)
    ).astype(jnp.bfloat16)
    grad_act = jnp.einsum("cin,kn->cki", cot_cells, out_weight, preferred_element_type=jnp.float32)
    sigmoid_m = jax.nn.sigmoid(message)
    grad_msg = (grad_act * sigmoid_m * (1.0 + message * (1.0 - sigmoid_m))).astype(jnp.bfloat16)
    grad_proj = return_partials(grad_msg, tile_stack, radial_weight)
    feature_grad = (
        cot_cells.astype(jnp.float32)
        + jnp.einsum(
            "cki,nk->cin",
            grad_proj.astype(jnp.bfloat16),
            proj_weight,
            preferred_element_type=jnp.float32,
        )
    ).astype(jnp.bfloat16)
    return (updated[None, :, None], feature_grad[None, :, None])


def solution(mesh):
    placed = (
        P("xy", None, "gz", None, None),
        P("xy", None, "gz", None, None),
        P("xy", None, "gz", None, None),
        P("xy", None, "gz"),
        P("xy", None, "gz", None),
        P(),
        P(),
        P(),
    )
    return jax.shard_map(
        on_device,
        mesh=mesh,
        in_specs=placed,
        out_specs=(P("xy", None, "gz", None, None), P("xy", None, "gz", None, None)),
        check_vma=False,
    )
```

profile of v0, /device:TPU:0, one launch (start us, length us, event | category | flops | bytes accessed | tf_op | source)
XLA Modules:
  0.0 391.7 jit_solution(9345513396120256922)
XLA Ops:
  3.3 2.9 collective-permute-start.5
  7.2 2.6 collective-permute-start.1
  9.9 2.3 collective-permute-start.6
  12.2 2.1 collective-permute-start.7
  14.3 1.7 collective-permute-done.6
  16.2 1.5 collective-permute-start.2
  17.6 2.5 collective-permute-start.3
  20.2 248.6 %while.52 = (s32[]{:T(128)}, bf16[27,2,8,64,64]{4,3,1,2,0:T(8,128)(2,1)}, s32[27]{0:T(128)S(1)}, f32[3,2,3,5,64]{4,1,3,2,0:T(2,128)S(1)}, f32[2,5,64]{2,0,1:T(2,...) while((s32[]{:T(128)}, ...), condition=%wide.region_2.3_spmd, body=%wide.region_0.2_spmd.sunk | while | flops 996423 | bytes 1491816 | solution.py:76
  268.9 66.6 %while.54 = (s32[]{:T(128)}, f32[2,64,64]{2,1,0:T(8,128)S(1)}, bf16[3,2,3,64,64]{4,3,1,2,0:T(8,128)(2,1)S(1)}, bf16[27,2,8,64,64]{4,3,1,2,0:T(8,128)(2,1)}, f32[...) while((s32[]{:T(128)}, f32[2,64,64]{2,1,0:T(8,128)S(1)}, ...), condition=%wide.region_4.5_spmd.clone, body=%wide.region_3.4_spmd.clone.sunk | while | flops 9224243 | bytes 973952 | solution.py:95
  269.0 1.3 convolution_bitcast_fusion.4
  271.5 1.3 convolution_bitcast_fusion.4
  274.0 1.3 convolution_bitcast_fusion.4
  276.4 1.3 convolution_bitcast_fusion.4
  281.4 1.3 convolution_bitcast_fusion.4
  283.8 1.3 convolution_bitcast_fusion.4
  286.3 1.3 convolution_bitcast_fusion.4
  288.8 1.3 convolution_bitcast_fusion.4
  291.2 1.3 convolution_bitcast_fusion.4
  293.7 1.3 convolution_bitcast_fusion.4
  298.6 1.3 convolution_bitcast_fusion.4
  301.1 1.3 convolution_bitcast_fusion.4
  303.6 1.3 convolution_bitcast_fusion.4
  306.0 1.3 convolution_bitcast_fusion.4
  311.0 1.3 convolution_bitcast_fusion.4
  313.4 1.3 convolution_bitcast_fusion.4
  315.9 1.3 convolution_bitcast_fusion.4
  318.4 1.3 convolution_bitcast_fusion.4
  320.8 1.3 convolution_bitcast_fusion.4
  335.8 43.9 %while.53 = (s32[]{:T(128)}, f32[3,2,3,64,64]{4,3,2,1,0:T(8,128)S(1)}, bf16[27,2,8,64,64]{4,3,1,2,0:T(8,128)(2,1)}, bf16[2,64,64]{2,1,0:T(8,128)(2,1)S(1)}, f32[...) while((s32[]{:T(128)}, ...), condition=%wide.region_6.7_spmd, body=%wide.region_5.6_spmd.sunk | while | flops 8527920 | bytes 969306 | solution.py:115
  379.8 3.8 collective-permute-start.9
  383.7 2.6 collective-permute-done.8
  386.4 2.6 collective-permute-start.11
  (864 shorter events, 157.5 us)
Async XLA Ops:
  0.6 334.9 %copy-start = (bf16[64,128]{1,0:T(8,128)(2,1)S(1)}, bf16[64,128]{1,0:T(8,128)(2,1)}, u32[]{:S(2)}) copy-start(bf16[64,128]{1,0:T(8,128)(2,1)} %param.20) | copy-start | bytes 49156
  0.6 268.2 %copy-start.1 = (f32[8,64]{1,0:T(8,128)S(1)}, f32[8,64]{1,0:T(8,128)}, u32[]{:S(2)}) copy-start(f32[8,64]{1,0:T(8,128)} %param.21) | copy-start | bytes 6148
  2.8 7.1 %collective-permute-start.4 = (f32[1,2,1,5,64]{4,1,3,2,0:T(2,128)S(1)}, f32[1,2,1,5,64]{4,1,3,2,0:T(2,128)S(1)}, u32[]{:S(2)}, u32[]{:S(2)}) collective-permute-start(f32[1,2,1,5,64]{4,1,3,2,0:T(2,128)S(1)} %pad_maximum_fusion.4), channel_id=1, source_target_pairs={{0,4},{4,8},{8,12},{12,16},{16,20},{20,24},{24,28},{28,0},{1,5},{5... | collective-permute-start | bytes 7688 | tf_op jit(solution)/shard_map/ppermute | solution.py:22
  3.3 6.5 %collective-permute-start.5 = (f32[1,2,1,5,64]{4,1,3,2,0:T(2,128)S(1)}, f32[1,2,1,5,64]{4,1,3,2,0:T(2,128)S(1)}, u32[]{:S(2)}, u32[]{:S(2)}) collective-permute-start(f32[1,2,1,5,64]{4,1,3,2,0:T(2,128)S(1)} %pad_maximum_fusion.4), channel_id=1, source_target_pairs={{4,0},{8,4},{12,8},{16,12},{20,16},{24,20},{28,24},{0,28},{5,1},{9... | collective-permute-start | bytes 7688 | tf_op jit(solution)/shard_map/ppermute | solution.py:23
  7.2 9.0 %collective-permute-start = (bf16[1,2,1,64,64]{4,3,1,2,0:T(8,128)(2,1)S(1)}, bf16[1,2,1,64,64]{4,3,1,2,0:T(8,128)(2,1)S(1)}, u32[]{:S(2)}, u32[]{:S(2)}) collective-permute-start(bf16[1,2,1,64,64]{4,3,1,2,0:T(8,128)(2,1)S(1)} %fusion.39), channel_id=1, source_target_pairs={{0,4},{4,8},{8,12},{12,16},{16,20},{20,24},{24,28},{28,0},{1,5},{5... | collective-permute-start | bytes 49160 | tf_op jit(solution)/shard_map/ppermute | solution.py:22
  7.2 8.9 %collective-permute-start.1 = (bf16[1,2,1,64,64]{4,3,1,2,0:T(8,128)(2,1)S(1)}, bf16[1,2,1,64,64]{4,3,1,2,0:T(8,128)(2,1)S(1)}, u32[]{:S(2)}, u32[]{:S(2)}) collective-permute-start(bf16[1,2,1,64,64]{4,3,1,2,0:T(8,128)(2,1)S(1)} %fusion.39), channel_id=1, source_target_pairs={{4,0},{8,4},{12,8},{16,12},{20,16},{24,20},{28,24},{0,28},{5,1},{9... | collective-permute-start | bytes 49160 | tf_op jit(solution)/shard_map/ppermute | solution.py:23
  9.9 6.2 %collective-permute-start.6 = (f32[3,2,1,5,64]{4,1,3,2,0:T(2,128)S(1)}, f32[3,2,1,5,64]{4,1,3,2,0:T(2,128)S(1)}, u32[]{:S(2)}, u32[]{:S(2)}) collective-permute-start(f32[3,2,1,5,64]{4,1,3,2,0:T(2,128)S(1)} %pad_maximum_fusion.3), channel_id=1, source_target_pairs={{0,1},{1,2},{2,3},{3,0},{4,5},{5,6},{6,7},{7,4},{8,9},{9,10},{10,1... | collective-permute-start | bytes 23048 | tf_op jit(solution)/shard_map/ppermute | solution.py:22
  12.2 3.9 collective-permute-start.7
  16.2 252.6 %collective-permute-start.2 = (bf16[3,2,1,64,64]{4,3,1,2,0:T(8,128)(2,1)S(1)}, bf16[3,2,1,64,64]{4,3,1,2,0:T(8,128)(2,1)S(1)}, u32[]{:S(2)}, u32[]{:S(2)}) collective-permute-start(bf16[3,2,1,64,64]{4,3,1,2,0:T(8,128)(2,1)S(1)} %pad_maximum_fusion.1), channel_id=1, source_target_pairs={{0,1},{1,2},{2,3},{3,0},{4,5},{5,6},{6,7},{7,4},{8,9},{9,10},{10,1... | collective-permute-start | bytes 147464 | tf_op jit(solution)/shard_map/ppermute | solution.py:22
  17.6 251.2 %collective-permute-start.3 = (bf16[3,2,1,64,64]{4,3,1,2,0:T(8,128)(2,1)S(1)}, bf16[3,2,1,64,64]{4,3,1,2,0:T(8,128)(2,1)S(1)}, u32[]{:S(2)}, u32[]{:S(2)}) collective-permute-start(bf16[3,2,1,64,64]{4,3,1,2,0:T(8,128)(2,1)S(1)} %pad_maximum_fusion.1), channel_id=1, source_target_pairs={{1,0},{2,1},{3,2},{0,3},{5,4},{6,5},{7,6},{4,7},{9,8},{10,9},{11,1... | collective-permute-start | bytes 147464 | tf_op jit(solution)/shard_map/ppermute | solution.py:23
  268.8 66.8 %copy-start.4 = (bf16[1,2,1,64,128]{4,3,2,1,0:T(8,128)(2,1)S(1)}, bf16[1,2,1,64,128]{4,3,2,1,0:T(8,128)(2,1)}, u32[]{:S(2)}) copy-start(bf16[1,2,1,64,128]{4,3,2,1,0:T(8,128)(2,1)} %param.15) | copy-start | bytes 98308
  335.5 53.5 %copy-start.3 = (bf16[1,2,1,64,128]{4,3,2,1,0:T(8,128)(2,1)S(1)}, bf16[1,2,1,64,128]{4,3,2,1,0:T(8,128)(2,1)}, u32[]{:S(2)}) copy-start(bf16[1,2,1,64,128]{4,3,2,1,0:T(8,128)(2,1)} %param.14) | copy-start | bytes 98308
  335.5 55.4 %copy-start.2 = (bf16[128,64]{0,1:T(8,128)(2,1)S(1)}, bf16[128,64]{0,1:T(8,128)(2,1)}, u32[]{:S(2)}) copy-start(bf16[128,64]{0,1:T(8,128)(2,1)} %param.19) | copy-start | bytes 49156
  379.8 6.5 %collective-permute-start.8 = (bf16[3,2,64,64]{3,2,1,0:T(8,128)(2,1)S(1)}, bf16[3,2,64,64]{3,2,1,0:T(8,128)(2,1)S(1)}, u32[]{:S(2)}, u32[]{:S(2)}) collective-permute-start(bf16[3,2,64,64]{3,2,1,0:T(8,128)(2,1)S(1)} %get-tuple-element.767), channel_id=1, source_target_pairs={{3,0},{0,1},{1,2},{2,3},{7,4},{4,5},{5,6},{6,7},{11,8},{8,9},{9,10... | collective-permute-start | bytes 147464 | tf_op jit(solution)/shard_map/ppermute | solution.py:12
  379.8 6.4 %collective-permute-start.9 = (bf16[3,2,64,64]{3,2,1,0:T(8,128)(2,1)S(1)}, bf16[3,2,64,64]{3,2,1,0:T(8,128)(2,1)S(1)}, u32[]{:S(2)}, u32[]{:S(2)}) collective-permute-start(bf16[3,2,64,64]{3,2,1,0:T(8,128)(2,1)S(1)} %get-tuple-element.768), channel_id=1, source_target_pairs={{1,0},{2,1},{3,2},{0,3},{5,4},{6,5},{7,6},{4,7},{9,8},{10,9},{11,1... | collective-permute-start | bytes 147464 | tf_op jit(solution)/shard_map/ppermute | solution.py:12
  386.3 4.6 %collective-permute-start.10 = (bf16[2,64,64]{2,1,0:T(8,128)(2,1)S(1)}, bf16[2,64,64]{2,1,0:T(8,128)(2,1)S(1)}, u32[]{:S(2)}, u32[]{:S(2)}) collective-permute-start(bf16[2,64,64]{2,1,0:T(8,128)(2,1)S(1)} %get-tuple-element.769), channel_id=1, source_target_pairs={{28,0},{0,4},{4,8},{8,12},{12,16},{16,20},{20,24},{24,28},{29,1},{... | collective-permute-start | bytes 49160 | tf_op jit(solution)/shard_map/ppermute | solution.py:12
  386.4 4.5 %collective-permute-start.11 = (bf16[2,64,64]{2,1,0:T(8,128)(2,1)S(1)}, bf16[2,64,64]{2,1,0:T(8,128)(2,1)S(1)}, u32[]{:S(2)}, u32[]{:S(2)}) collective-permute-start(bf16[2,64,64]{2,1,0:T(8,128)(2,1)S(1)} %get-tuple-element.770), channel_id=1, source_target_pairs={{4,0},{8,4},{12,8},{16,12},{20,16},{24,20},{28,24},{0,28},{5,1},{9... | collective-permute-start | bytes 49160 | tf_op jit(solution)/shard_map/ppermute | solution.py:12
where the time goes:
time: 396 us; the launch traced here: 392 us
  loops' own time  183 us (46%)
  local copies, waits for them, and re-layouts  72.9 us (18%)
  matrix products  68.5 us (17%)
  other arithmetic  39.4 us (10%)
  starting transfers between devices  21.1 us (5%)
  waiting for transfers between devices  5.49 us (1%)
    another operation x1, loops' own time, all_tiles(): return lax.map(one_direction, jnp.arange(27, dtype=jnp.int32))  176 us
    dot_general x27, matrix products, add_pair(): jnp.einsum('cbij,ckj->cbki', tile_set, other_source, preferred_element_ty...  35.8 us
    dynamic_slice x54, local copies, waits for them, and re-layouts, add_back(): lax.dynamic_index_in_dim(tile_stack, direction, 0, keepdims=False)  31 us
    dot_general x27, matrix products, add_pair(): jnp.einsum('cbki,bk->cki', per_basis, radial_weight, precision=lax.Precis...  24 us
    while x189, other arithmetic  20.3 us
    dynamic_update_slice x27, local copies, waits for them, and re-layouts, all_tiles(): return lax.map(one_direction, jnp.arange(27, dtype=jnp.int32))  19.8 us
    dynamic_slice x27, local copies, waits for them, and re-layouts, all_tiles(): return lax.map(one_direction, jnp.arange(27, dtype=jnp.int32))  15.9 us
    ppermute x4, starting transfers between devices, with_halo(): after = lax.ppermute(initial, axis, down)  10.2 us
  transfers between devices with their start and end apart: 12, of which 4 were waited for; matrix products, arithmetic and copies ran while one was open for 19% of the time, Pallas kernels for 0%

commit v1 on v0

v1 whole, which is shorter than its diff:
```python
import functools

import jax
import jax.numpy as jnp
from jax import lax
from jax.experimental import pallas as pl
from jax.experimental.pallas import tpu as pltpu
from jax.sharding import PartitionSpec as P

MESH = pl.DeviceIdType.MESH
AXES = ("xy", "gz")
CENTRE = 4
GROUPS = ((4,), (1, 7), (3, 5), (0, 2), (6, 8))
SLOT = {n: at for at, n in enumerate(n for group in GROUPS for n in group)}
F32 = jnp.float32
BF16 = jnp.bfloat16


def nt(a, b):
    return lax.dot_general(a, b, (((1,), (1,)), ((), ())), preferred_element_type=F32)


def tn(a, b):
    return lax.dot_general(a, b, (((0,), (0,)), ((), ())), preferred_element_type=F32)


def direction(column, oy):
    return column // 3 * 9 + (oy + 1) * 3 + column % 3


def kernel(
    atoms,
    bases,
    feat_ref,
    cot_ref,
    pos_ref,
    counts_ref,
    mask_ref,
    proj_ref,
    outw_ref,
    radial_ref,
    updated_ref,
    grad_ref,
    packet_out,
    packet_in,
    own_cols,
    tiles,
    source,
    grads,
    send_sem,
    recv_sem,
):
    rows = feat_ref.shape[0]
    sizes = [lax.axis_size(axis) for axis in AXES]
    here = [lax.axis_index(axis) for axis in AXES]
    others = [n for group in GROUPS for n in group if n != CENTRE]

    def device_at(column):
        ox, oz = column // 3 - 1, column % 3 - 1
        return (lax.rem(here[0] + ox + sizes[0], sizes[0]), lax.rem(here[1] + oz + sizes[1], sizes[1]))

    barrier = pltpu.get_barrier_semaphore()
    for n in others:
        pl.semaphore_signal(barrier, inc=1, device_id=device_at(n), device_id_type=MESH)

    lane = lax.broadcasted_iota(jnp.int32, (1, rows), 1)
    upper = lane >= atoms
    valid_lane = (lane - jnp.where(upper, atoms, 0)) < jnp.where(upper, counts_ref[1], counts_ref[0])
    valid_row = valid_lane.astype(F32)

    def lanes_of(n):
        return pl.ds(SLOT[n] * rows, rows)

    projected = lax.dot_general(
        proj_ref[...], feat_ref[...], (((0,), (1,)), ((), ())), preferred_element_type=F32
    )
    source[:, lanes_of(CENTRE)] = (projected * valid_row).astype(BF16)

    place = 2.0 * jnp.concatenate([pos_ref[0], pos_ref[1]], axis=-1)
    for m in range(9):
        listed = [
            jnp.where(
                upper,
                mask_ref[1, direction(m, -oy)].astype(F32),
                mask_ref[0, direction(m, -oy)].astype(F32),
            )
            for oy in (-1, 0, 1)
        ]
        packet = jnp.concatenate([place] + listed + [jnp.zeros((2, rows), F32)], axis=0)
        packet_out[m] = packet
        if m == CENTRE:
            packet_in[CENTRE] = packet
            columns = packet.T
            for axis in range(3):
                own_cols[axis] = jnp.broadcast_to(columns[:, axis : axis + 1], (rows, rows))

    def copies(kind):
        made = {}
        for m in others:
            n = 8 - m
            if kind == 0:
                src, dst = packet_out.at[m], packet_in.at[n]
            else:
                held = source if kind == 1 else grads
                src, dst = held.at[:, lanes_of(CENTRE)], held.at[:, lanes_of(n)]
            made[n] = pltpu.make_async_remote_copy(
                src_ref=src,
                dst_ref=dst,
                send_sem=send_sem.at[kind, n],
                recv_sem=recv_sem.at[kind, n],
                device_id=device_at(m),
                device_id_type=MESH,
            )
        return made

    def build(n):
        ox, oz = n // 3 - 1, n % 3 - 1
        packet = packet_in[n]
        other_x = packet[0:1] + 2.0 * ox
        other_y = packet[1:2]
        other_z = packet[2:3] + 2.0 * oz
        chunk = 32
        for c in range(2):
            cross = upper if c == 0 else jnp.logical_not(upper)
            low, same, high = (
                packet[4 + oy : 5 + oy] * mask_ref[c, direction(n, oy)].astype(F32)
                for oy in (-1, 0, 1)
            )
            gate_low = jnp.where(cross, low, same)
            gate_high = jnp.where(cross, high, same)
            move_low = jnp.where(cross, -2.0, 0.0)
            move_high = jnp.where(cross, 2.0, 0.0)

            def part(step, carry):
                first = pl.multiple_of(c * atoms + step * chunk, chunk)
                some = pl.ds(first, chunk)
                dx = other_x - own_cols[0, some, :]
                dy = other_y - own_cols[1, some, :]
                dz = other_z - own_cols[2, some, :]
                above = dy > 0.0
                dy = dy + jnp.where(above, move_low, move_high)
                gate = jnp.where(above, gate_low, gate_high)
                near = jnp.minimum(dx * dx + dy * dy + dz * dz, 1.0)
                room = 1.0 - near
                envelope = room * room * gate
                if n == CENTRE:
                    at_row = lax.broadcasted_iota(jnp.int32, (chunk, rows), 0) + first
                    at_lane = lax.broadcasted_iota(jnp.int32, (chunk, rows), 1)
                    envelope = jnp.where(at_row == at_lane, 0.0, envelope)
                half = bases // 2
                v = bases * near - half
                up = jnp.exp(2.0 * v)
                down = jnp.exp(-2.0 * v)
                middle = envelope * jnp.exp(-2.0 * (v * v) - 0.5)
                up2, down2 = up * up, down * down
                high_value, low_value = middle * up, middle * down
                for step_out in range(half):
                    if step_out:
                        fall = EXP_FALL[step_out]
                        high_value = high_value * (up2 * fall)
                        low_value = low_value * (down2 * fall)
                    for b, value in ((half + step_out, high_value), (half - 1 - step_out, low_value)):
                        tiles[b, some, lanes_of(n)] = value.astype(BF16)
                return carry

            lax.fori_loop(0, atoms // chunk, part, 0)

    def gathered(held, group, total):
        width = len(group) * rows
        span = pl.ds(SLOT[group[0]] * rows, width)
        stack = tiles[:, :, span].reshape(bases * rows, width)
        sums = nt(stack, held[:, span])
        for b in range(bases):
            term = sums[b * rows : (b + 1) * rows] * radial_ref[b : b + 1, :]
            total = term if total is None else total + term
        return total

    pl.semaphore_wait(barrier, len(others))
    packets = copies(0)
    sources = copies(1)
    for n in others:
        packets[8 - n].start()
    for n in others:
        sources[8 - n].start()

    build(CENTRE)
    message = gathered(source, GROUPS[0], None)
    grad_act = nt(outw_ref[...], cot_ref[...])
    for group in GROUPS[1:]:
        for n in group:
            packets[n].wait_recv()
            build(n)
    for group in GROUPS[1:]:
        for n in group:
            sources[n].wait_recv()
        message = gathered(source, group, message)

    message = message.T * valid_row
    gate = 1.0 / (1.0 + jnp.exp(-message))
    grad_msg = grad_act * gate * (1.0 + message * (1.0 - gate)) * valid_row
    grads[:, lanes_of(CENTRE)] = grad_msg.astype(BF16)
    returns = copies(2)
    for n in others:
        returns[8 - n].start()

    activated = (message * gate).astype(BF16)
    updated_ref[...] = (feat_ref[...].astype(F32) + tn(activated, outw_ref[...])).astype(BF16)

    total = gathered(grads, GROUPS[0], None)
    for group in GROUPS[1:]:
        for n in group:
            returns[n].wait_recv()
        total = gathered(grads, group, total)
    at_row = lax.broadcasted_iota(jnp.int32, total.shape, 0)
    in_upper = at_row >= atoms
    kept = (at_row - jnp.where(in_upper, atoms, 0)) < jnp.where(in_upper, counts_ref[1], counts_ref[0])
    grad_proj = jnp.where(kept, total, 0.0).astype(BF16)
    grad_ref[...] = (cot_ref[...].astype(F32) + nt(grad_proj, proj_ref[...])).astype(BF16)

    for made in (packets, sources, returns):
        for n in others:
            made[n].wait_send()


EXP_FALL = [2.718281828459045 ** (-4.0 * step) for step in range(8)]


def on_device(
    features, cotangent, positions, counts, neighbour_mask, proj_weight, out_weight, radial_weight
):
    shape = features.shape
    cells, atoms, channels = shape[1], shape[3], shape[4]
    bases, width = radial_weight.shape
    rows = cells * atoms
    assert shape[0] == 1 and shape[2] == 1 and cells == 2
    vmem = pl.BlockSpec(memory_space=pltpu.VMEM)
    smem = pl.BlockSpec(memory_space=pltpu.SMEM)
    updated, grad = pl.pallas_call(
        functools.partial(kernel, atoms, bases),
        out_shape=[jax.ShapeDtypeStruct((rows, channels), BF16)] * 2,
        in_specs=[vmem, vmem, vmem, smem, smem, vmem, vmem, vmem],
        out_specs=[vmem, vmem],
        scratch_shapes=[
            pltpu.VMEM((9, 8, rows), F32),
            pltpu.VMEM((9, 8, rows), F32),
            pltpu.VMEM((3, rows, rows), F32),
            pltpu.VMEM((bases, rows, 9 * rows), BF16),
            pltpu.VMEM((width, 9 * rows), BF16),
            pltpu.VMEM((width, 9 * rows), BF16),
            pltpu.SemaphoreType.DMA((3, 9)),
            pltpu.SemaphoreType.DMA((3, 9)),
        ],
        compiler_params=pltpu.CompilerParams(collective_id=0, has_side_effects=True),
    )(
        features.reshape(rows, channels),
        cotangent.reshape(rows, channels),
        positions.reshape(cells, 3, atoms),
        counts.reshape(cells),
        neighbour_mask.reshape(cells, neighbour_mask.shape[-1]),
        proj_weight,
        out_weight,
        radial_weight,
    )
    return updated.reshape(shape), grad.reshape(shape)


def solution(mesh):
    cell = P("xy", None, "gz", None, None)
    return jax.shard_map(
        on_device,
        mesh=mesh,
        in_specs=(cell, cell, cell, P("xy", None, "gz"), P("xy", None, "gz", None), P(), P(), P()),
        out_specs=(cell, cell),
        check_vma=False,
    )
```

time: 396 us -> 25.4 us (0.06); the launches traced: 392 us -> 25.1 us
  loops' own time: 183 us -> 0 us
  local copies, waits for them, and re-layouts: 72.9 us -> 4.01 us
  matrix products: 68.5 us -> 0 us
  other arithmetic: 39.4 us -> 0 us
  starting transfers between devices: 21.1 us -> 0 us
  Pallas kernels: 0 us -> 20.4 us
  waiting for transfers between devices: 5.49 us -> 0 us
    another operation x3 -> x0, loops' own time: 183 us -> none  [the longest x1 176 us: all_tiles(): return lax.map(one_direction, jnp.arange(27, dtype=jnp.int32))]
    dot_general x85 -> x0, matrix products: 68.5 us -> none  [the longest x27 35.8 us: add_pair(): jnp.einsum('cbij,ckj->cbki', tile_set, other_source, preferred_element_ty...]
    dynamic_slice x81 -> x0, local copies, waits for them, and re-layouts: 46.9 us -> none  [the longest x54 31 us: add_back(): lax.dynamic_index_in_dim(tile_stack, direction, 0, keepdims=False)]
    ppermute x12 -> x0, starting transfers between devices: 21.1 us -> none  [the longest x4 10.2 us: with_halo(): after = lax.ppermute(initial, axis, down)]
    pallas_call x0 -> x1, Pallas kernels: none -> 20.4 us  [on_device(): pl.pallas_call(functools.partial(kernel, atoms, bases), out_shape=[jax.Sh...]
    while x189 -> x0, other arithmetic: 20.3 us -> none
    dynamic_update_slice x27 -> x0, local copies, waits for them, and re-layouts: 19.8 us -> none  [all_tiles(): return lax.map(one_direction, jnp.arange(27, dtype=jnp.int32))]
    ppermute x12 -> x0, waiting for transfers between devices: 5.49 us -> none  [the longest x4 3.69 us: shifted(): return lax.ppermute(block, axis, route)]
  transfers between devices with their start and end apart: 12 -> 0, of which waited for: 4 -> 0; matrix products, arithmetic and copies ran while one was open for 19% -> 0% of each run, Pallas kernels for 0% -> 0%
where the time goes in v1:
time: 25.4 us; the launch traced here: 25.1 us
  Pallas kernels  20.4 us (80%)
  local copies, waits for them, and re-layouts  4.01 us (16%)
  between operations  0.66 us (3%)
    pallas_call x1, Pallas kernels, on_device(): pl.pallas_call(functools.partial(kernel, atoms, bases), out_shape=[jax.Sh...  20.4 us
    unnamed x8, local copies, waits for them, and re-layouts  3.42 us
    reshape x1, local copies, waits for them, and re-layouts, on_device(): positions.reshape(cells, 3, atoms)  0.6 us

profile of v1, /device:TPU:0, one launch (start us, length us, event | category | flops | bytes accessed | tf_op | source)
XLA Modules:
  0.0 25.1 jit_solution(18352285409654540658)
XLA Ops:
  0.6 0.0 copy-start.1
  0.6 0.7 %copy.19 = f32[1,2,1,3,64]{4,1,3,2,0:T(2,128)S(1)} copy(f32[1,2,1,3,64]{4,2,3,1,0:T(1,128)} %param.10) | data formatting | bytes 3072 | tf_op args[2]
  1.3 0.6 %copy.14.pos_ref = f32[2,3,64]{2,1,0:T(4,128)} copy(f32[2,3,64]{2,0,1:T(2,128)S(1)} %bitcast.17) | data formatting | bytes 3072 | tf_op jit(solution)/shard_map/reshape | solution.py:257
  1.9 0.0 copy-done.1
  1.9 0.7 %copy.15.proj_ref = bf16[128,64]{1,0:T(8,128)(2,1)} copy(bf16[128,64]{0,1:T(8,128)(2,1)S(1)} %copy-done.1) | data formatting | bytes 32768 | tf_op args[5]
  2.7 20.4 %shard_map.95 = (bf16[128,128]{1,0:T(8,128)(2,1)}, bf16[128,128]{1,0:T(8,128)(2,1)}) custom-call(bf16[128,128]{1,0:T(8,128)(2,1)} %bitcast.15, bf16[128,128]{1,0:T(8,128)(2,1)} %bitcast.16, f32[2,3,64]{2,1,0:T(4,128)} %copy.14.pos_ref, s32[2]{0:T(128)} %bitcast.19, s32[2,27]{1,0:T(2,128)} %bitcast.18, bf16[128,64]{1,0:T(8,128)(2,1)} %copy.15.proj_ref, ...), custom_call_target="tpu_custom_call" | custom-call | tf_op jit(solution)/shard_map/pallas_call | solution.py:238
  23.1 0.0 copy-start
  23.1 1.4 %copy.22 = bf16[1,2,1,64,128]{4,3,2,1,0:T(8,128)(2,1)} copy(bf16[1,2,1,64,128]{4,3,2,1,0:T(8,128)(2,1)} %bitcast.14) | data formatting | bytes 65536
  24.5 0.0 copy-done
  24.5 0.6 %copy.23 = bf16[1,2,1,64,128]{4,3,2,1,0:T(8,128)(2,1)} copy(bf16[1,2,1,64,128]{4,3,2,1,0:T(8,128)(2,1)S(1)} %bitcast.13) | data formatting | bytes 65536
Async XLA Ops:
  0.6 1.3 %copy-start.1 = (bf16[128,64]{0,1:T(8,128)(2,1)S(1)}, bf16[128,64]{0,1:T(8,128)(2,1)}, u32[]{:S(2)}) copy-start(bf16[128,64]{0,1:T(8,128)(2,1)} %param.13) | copy-start | bytes 49156
  23.1 1.4 %copy-start = (bf16[128,128]{1,0:T(8,128)(2,1)S(1)}, bf16[128,128]{1,0:T(8,128)(2,1)}, u32[]{:S(2)}) copy-start(bf16[128,128]{1,0:T(8,128)(2,1)} %get-tuple-element.5) | copy-start | bytes 98308

commit v2 on v1

v2 whole, which is shorter than its diff:
```python
import functools

import jax
import jax.numpy as jnp
from jax import lax
from jax.experimental import pallas as pl
from jax.experimental.pallas import tpu as pltpu
from jax.sharding import PartitionSpec as P

MESH = pl.DeviceIdType.MESH
AXES = ("xy", "gz")
GROUPS = (((0, 0),), ((-1, 0), (1, 0)), ((0, -1), (0, 1)), ((-1, -1), (-1, 1)), ((1, -1), (1, 1)))
SLOT = {at: slot for slot, at in enumerate(at for group in GROUPS for at in group)}
F32 = jnp.float32
BF16 = jnp.bfloat16


def nt(a, b):
    return lax.dot_general(a, b, (((1,), (1,)), ((), ())), preferred_element_type=F32)


def tn(a, b):
    return lax.dot_general(a, b, (((0,), (0,)), ((), ())), preferred_element_type=F32)


def direction(ox, oy, oz):
    return (ox + 1) * 9 + (oy + 1) * 3 + oz + 1


def kernel(
    atoms,
    bases,
    feat_hbm,
    cot_hbm,
    pos_hbm,
    counts_hbm,
    mask_hbm,
    proj_hbm,
    outw_hbm,
    radial_hbm,
    updated_hbm,
    grad_hbm,
    feat_ref,
    cot_ref,
    pos_ref,
    counts_ref,
    mask_ref,
    proj_ref,
    outw_ref,
    radial_ref,
    updated_ref,
    grad_ref,
    packet_out,
    packet_in,
    own_cols,
    tiles,
    source,
    grads,
    local_sem,
    send_sem,
    recv_sem,
):
    rows = feat_ref.shape[0]
    sizes = [lax.axis_size(axis) for axis in AXES]
    here = [lax.axis_index(axis) for axis in AXES]

    def device_at(ox, oz):
        return (lax.rem(here[0] + ox + sizes[0], sizes[0]), lax.rem(here[1] + oz + sizes[1], sizes[1]))

    barrier = pltpu.get_barrier_semaphore()
    beside = ((0, -1), (0, 1), (-1, 0), (1, 0))
    for ox, oz in beside:
        pl.semaphore_signal(barrier, inc=1, device_id=device_at(ox, oz), device_id_type=MESH)

    fetches = [
        pltpu.make_async_copy(far, near, local_sem.at[at])
        for at, (far, near) in enumerate(
            (
                (mask_hbm, mask_ref),
                (counts_hbm, counts_ref),
                (pos_hbm, pos_ref),
                (proj_hbm, proj_ref),
                (feat_hbm, feat_ref),
                (radial_hbm, radial_ref),
                (outw_hbm, outw_ref),
                (cot_hbm, cot_ref),
            )
        )
    ]
    for fetch in fetches:
        fetch.start()
    for fetch in fetches[:5]:
        fetch.wait()

    lane = lax.broadcasted_iota(jnp.int32, (1, rows), 1)
    upper = lane >= atoms
    valid_lane = (lane - jnp.where(upper, atoms, 0)) < jnp.where(upper, counts_ref[1], counts_ref[0])
    valid_row = valid_lane.astype(F32)

    def lanes_of(slot):
        first = slot * rows
        return pl.ds(first if isinstance(slot, int) else pl.multiple_of(first, rows), rows)

    place = 2.0 * jnp.concatenate(
        [
            jnp.concatenate([pos_ref[axis], pos_ref[3 + axis]], axis=-1)
            for axis in range(3)
        ],
        axis=0,
    )
    for oz in (-1, 0, 1):
        listed = [
            jnp.where(
                upper,
                mask_ref[1, direction(ox, -oy, oz)].astype(F32),
                mask_ref[0, direction(ox, -oy, oz)].astype(F32),
            )
            for ox in (-1, 0, 1)
            for oy in (-1, 0, 1)
        ]
        packet = jnp.concatenate([place] + listed + [jnp.zeros((4, rows), F32)], axis=0)
        packet_out[oz + 1] = packet
        if oz == 0:
            packet_in[0] = packet
    columns = jnp.concatenate([place, jnp.zeros((5, rows), F32)], axis=0).T
    for axis in range(3):
        own_cols[axis] = jnp.broadcast_to(columns[:, axis : axis + 1], (rows, rows))

    projected = nt(proj_ref[...], feat_ref[...])
    source[:, lanes_of(0)] = (projected * valid_row).astype(BF16)

    def held_at(kind, slot):
        if kind == 0:
            return packet_in.at[slot]
        return (source if kind == 1 else grads).at[:, lanes_of(slot)]

    def send(kind, src, slot, ox, oz):
        return pltpu.make_async_remote_copy(
            src_ref=src,
            dst_ref=held_at(kind, slot),
            send_sem=send_sem.at[kind, slot],
            recv_sem=recv_sem.at[kind, slot],
            device_id=device_at(ox, oz),
            device_id_type=MESH,
        )

    started = []

    def spread(kind):
        for ox, oz in beside:
            src = packet_out.at[oz + 1] if kind == 0 else held_at(kind, 0)
            copy = send(kind, src, SLOT[-ox, -oz], ox, oz)
            copy.start()
            started.append(copy)

    def arrived(kind, slot):
        send(kind, held_at(kind, slot), slot, 1, 0).wait_recv()

    def forward(kind, at):
        arrived(kind, 3 + at)
        for ox in (-1, 1):
            copy = send(kind, held_at(kind, 3 + at), SLOT[-ox, -1] + at, ox, 0)
            copy.start()
            started.append(copy)

    sooner = jnp.where(here[1] == 0, 1, 0)
    later = 1 - sooner

    def build(ox, oz):
        slot = SLOT[ox, oz]
        packet = packet_in[slot]
        other_x = packet[0:1] + 2.0 * ox
        other_y = packet[1:2]
        other_z = packet[2:3] + 2.0 * oz
        middle_row = 7 - 3 * ox
        chunk = 32
        for c in range(2):
            cross = upper if c == 0 else jnp.logical_not(upper)
            low, same, high = (
                packet[middle_row + oy : middle_row + oy + 1]
                * mask_ref[c, direction(ox, oy, oz)].astype(F32)
                for oy in (-1, 0, 1)
            )
            gate_low = jnp.where(cross, low, same)
            gate_high = jnp.where(cross, high, same)
            move_low = jnp.where(cross, -2.0, 0.0)
            move_high = jnp.where(cross, 2.0, 0.0)

            def part(step, carry):
                first = pl.multiple_of(c * atoms + step * chunk, chunk)
                some = pl.ds(first, chunk)
                dx = other_x - own_cols[0, some, :]
                dy = other_y - own_cols[1, some, :]
                dz = other_z - own_cols[2, some, :]
                above = dy > 0.0
                dy = dy + jnp.where(above, move_low, move_high)
                gate = jnp.where(above, gate_low, gate_high)
                near = jnp.minimum(dx * dx + dy * dy + dz * dz, 1.0)
                room = 1.0 - near
                envelope = room * room * gate
                if slot == 0:
                    at_row = lax.broadcasted_iota(jnp.int32, (chunk, rows), 0) + first
                    at_lane = lax.broadcasted_iota(jnp.int32, (chunk, rows), 1)
                    envelope = jnp.where(at_row == at_lane, 0.0, envelope)
                half = bases // 2
                v = bases * near - half
                up = jnp.exp(2.0 * v)
                down = jnp.exp(-2.0 * v)
                middle = envelope * jnp.exp(-2.0 * (v * v) - 0.5)
                up2, down2 = up * up, down * down
                high_value, low_value = middle * up, middle * down
                for step_out in range(half):
                    if step_out:
                        fall = EXP_FALL[step_out]
                        high_value = high_value * (up2 * fall)
                        low_value = low_value * (down2 * fall)
                    for b, value in ((half + step_out, high_value), (half - 1 - step_out, low_value)):
                        tiles[b, some, lanes_of(slot)] = value.astype(BF16)
                return carry

            lax.fori_loop(0, atoms // chunk, part, 0)

    def gathered(held, group, total):
        width = len(group) * rows
        span = pl.ds(SLOT[group[0]] * rows, width)
        stack = tiles[:, :, span].reshape(bases * rows, width)
        sums = nt(stack, held[:, span])
        for b in range(bases):
            term = sums[b * rows : (b + 1) * rows] * radial_ref[b : b + 1, :]
            total = term if total is None else total + term
        return total

    pl.semaphore_wait(barrier, len(beside))
    spread(0)
    spread(1)

    for fetch in fetches[5:]:
        fetch.wait()
    build(0, 0)
    message = gathered(source, GROUPS[0], None)
    grad_act = nt(outw_ref[...], cot_ref[...])
    forward(0, sooner)
    forward(1, sooner)
    for at in GROUPS[1]:
        arrived(0, SLOT[at])
        build(*at)
    for at in GROUPS[1]:
        arrived(1, SLOT[at])
    message = gathered(source, GROUPS[1], message)
    forward(0, later)
    forward(1, later)
    for at in GROUPS[2]:
        build(*at)
    message = gathered(source, GROUPS[2], message)
    for group in GROUPS[3:]:
        for at in group:
            arrived(0, SLOT[at])
            build(*at)
    for group in GROUPS[3:]:
        for at in group:
            arrived(1, SLOT[at])
        message = gathered(source, group, message)

    message = message.T * valid_row
    gate = 1.0 / (1.0 + jnp.exp(-message))
    grad_msg = grad_act * gate * (1.0 + message * (1.0 - gate)) * valid_row
    grads[:, lanes_of(0)] = grad_msg.astype(BF16)
    spread(2)

    activated = (message * gate).astype(BF16)
    updated_ref[...] = (feat_ref[...].astype(F32) + tn(activated, outw_ref[...])).astype(BF16)
    put_updated = pltpu.make_async_copy(updated_ref, updated_hbm, local_sem.at[8])
    put_updated.start()

    total = gathered(grads, GROUPS[0], None)
    forward(2, sooner)
    for at in GROUPS[1]:
        arrived(2, SLOT[at])
    total = gathered(grads, GROUPS[1], total)
    forward(2, later)
    for group in GROUPS[2:]:
        if group != GROUPS[2]:
            for at in group:
                arrived(2, SLOT[at])
        total = gathered(grads, group, total)
    at_row = lax.broadcasted_iota(jnp.int32, total.shape, 0)
    in_upper = at_row >= atoms
    kept = (at_row - jnp.where(in_upper, atoms, 0)) < jnp.where(in_upper, counts_ref[1], counts_ref[0])
    grad_proj = jnp.where(kept, total, 0.0).astype(BF16)
    pulled = jnp.dot(grad_proj, proj_ref[...], preferred_element_type=F32)
    grad_ref[...] = (cot_ref[...].astype(F32) + pulled).astype(BF16)
    put_grad = pltpu.make_async_copy(grad_ref, grad_hbm, local_sem.at[9])
    put_grad.start()

    for copy in started:
        copy.wait_send()
    put_updated.wait()
    put_grad.wait()


EXP_FALL = [2.718281828459045 ** (-4.0 * step) for step in range(8)]


def on_device(
    features, cotangent, positions, counts, neighbour_mask, proj_weight, out_weight, radial_weight
):
    shape = features.shape
    cells, atoms, channels = shape[1], shape[3], shape[4]
    bases, width = radial_weight.shape
    rows = cells * atoms
    assert shape[0] == 1 and shape[2] == 1 and cells == 2
    operands = (
        features.reshape(rows, channels),
        cotangent.reshape(rows, channels),
        positions.reshape(cells * 3, 1, atoms),
        counts.reshape(cells),
        neighbour_mask.reshape(cells, neighbour_mask.shape[-1]),
        proj_weight.T,
        out_weight,
        radial_weight,
    )
    held = [pltpu.SMEM if at in (3, 4) else pltpu.VMEM for at in range(len(operands))]
    updated, grad = pl.pallas_call(
        functools.partial(kernel, atoms, bases),
        out_shape=[jax.ShapeDtypeStruct((rows, channels), BF16)] * 2,
        in_specs=[pl.BlockSpec(memory_space=pl.ANY)] * len(operands),
        out_specs=[pl.BlockSpec(memory_space=pl.ANY)] * 2,
        scratch_shapes=[space(x.shape, x.dtype) for space, x in zip(held, operands)]
        + [
            pltpu.VMEM((rows, channels), BF16),
            pltpu.VMEM((rows, channels), BF16),
            pltpu.VMEM((3, 16, rows), F32),
            pltpu.VMEM((9, 16, rows), F32),
            pltpu.VMEM((3, rows, rows), F32),
            pltpu.VMEM((bases, rows, 9 * rows), BF16),
            pltpu.VMEM((width, 9 * rows), BF16),
            pltpu.VMEM((width, 9 * rows), BF16),
            pltpu.SemaphoreType.DMA((10,)),
            pltpu.SemaphoreType.DMA((3, 9)),
            pltpu.SemaphoreType.DMA((3, 9)),
        ],
        compiler_params=pltpu.CompilerParams(collective_id=0, has_side_effects=True),
    )(*operands)
    return updated.reshape(shape), grad.reshape(shape)


def solution(mesh):
    cell = P("xy", None, "gz", None, None)
    return jax.shard_map(
        on_device,
        mesh=mesh,
        in_specs=(cell, cell, cell, P("xy", None, "gz"), P("xy", None, "gz", None), P(), P(), P()),
        out_specs=(cell, cell),
        check_vma=False,
    )
```

time: 25.4 us -> 23.8 us (0.937)
  local copies, waits for them, and re-layouts: 4.01 us -> 2 us
  Pallas kernels: 20.4 us -> 20.9 us
    unnamed x8 -> x4, local copies, waits for them, and re-layouts: 3.42 us -> 2 us
    reshape x1 -> x0, local copies, waits for them, and re-layouts: 0.6 us -> none  [on_device(): positions.reshape(cells, 3, atoms)]
    pallas_call x1, Pallas kernels: 20.4 us -> 20.9 us  [on_device(): pl.pallas_call(functools.partial(kernel, atoms, bases), out_shape=[jax.Sh...]
where the time goes in v2:
time: 23.8 us; the launch traced here: 23.5 us
  Pallas kernels  20.9 us (88%)
  local copies, waits for them, and re-layouts  2 us (8%)
  between operations  0.65 us (3%)
    pallas_call x1, Pallas kernels, on_device(): pl.pallas_call(functools.partial(kernel, atoms, bases), out_shape=[jax.Sh...  20.9 us
    unnamed x4, local copies, waits for them, and re-layouts  2 us

profile of v2, /device:TPU:0, one launch (start us, length us, event | category | flops | bytes accessed | tf_op | source)
XLA Modules:
  0.0 23.5 jit_solution(5676498683502730361)
XLA Ops:
  0.6 20.9 %shard_map.95 = (bf16[128,128]{1,0:T(8,128)(2,1)}, bf16[128,128]{1,0:T(8,128)(2,1)}) custom-call(bf16[128,128]{1,0:T(8,128)(2,1)} %bitcast.12, bf16[128,128]{1,0:T(8,128)(2,1)} %bitcast.13, f32[6,1,64]{2,1,0:T(1,128)} %bitcast.17, s32[2]{0:T(128)} %bitcast.19, s32[2,27]{1,0:T(2,128)} %bitcast.18, bf16[64,128]{1,0:T(8,128)(2,1)} %bitcast.16, ...), custom_call_target="tpu_custom_call" | custom-call | tf_op jit(solution)/shard_map/pallas_call | solution.py:323
  21.5 0.0 copy-start
  21.5 1.4 %copy.14 = bf16[1,2,1,64,128]{4,3,2,1,0:T(8,128)(2,1)} copy(bf16[1,2,1,64,128]{4,3,2,1,0:T(8,128)(2,1)} %bitcast.15) | data formatting | bytes 65536
  22.9 0.0 copy-done
  22.9 0.6 %copy.15 = bf16[1,2,1,64,128]{4,3,2,1,0:T(8,128)(2,1)} copy(bf16[1,2,1,64,128]{4,3,2,1,0:T(8,128)(2,1)S(1)} %bitcast.14) | data formatting | bytes 65536
Async XLA Ops:
  21.5 1.4 %copy-start = (bf16[128,128]{1,0:T(8,128)(2,1)S(1)}, bf16[128,128]{1,0:T(8,128)(2,1)}, u32[]{:S(2)}) copy-start(bf16[128,128]{1,0:T(8,128)(2,1)} %get-tuple-element.5) | copy-start | bytes 98308

commit v3 on v2

--- a/solution.py
+++ b/solution.py
@@ -38,8 +38,8 @@
     proj_hbm,
     outw_hbm,
     radial_hbm,
-    updated_hbm,
-    grad_hbm,
+    updated_ref,
+    grad_ref,
     feat_ref,
     cot_ref,
     pos_ref,
@@ -48,8 +48,6 @@
     proj_ref,
     outw_ref,
     radial_ref,
-    updated_ref,
-    grad_ref,
     packet_out,
     packet_in,
     own_cols,
@@ -68,8 +66,8 @@
         return (lax.rem(here[0] + ox + sizes[0], sizes[0]), lax.rem(here[1] + oz + sizes[1], sizes[1]))
 
     barrier = pltpu.get_barrier_semaphore()
-    beside = ((0, -1), (0, 1), (-1, 0), (1, 0))
-    for ox, oz in beside:
+    others = [at for at, slot in SLOT.items() if slot]
+    for ox, oz in others[::-1]:
         pl.semaphore_signal(barrier, inc=1, device_id=device_at(ox, oz), device_id_type=MESH)
 
     fetches = [
@@ -108,19 +106,18 @@
         ],
         axis=0,
     )
-    for oz in (-1, 0, 1):
+    for (ox, oz), slot in SLOT.items():
         listed = [
             jnp.where(
                 upper,
                 mask_ref[1, direction(ox, -oy, oz)].astype(F32),
                 mask_ref[0, direction(ox, -oy, oz)].astype(F32),
             )
-            for ox in (-1, 0, 1)
             for oy in (-1, 0, 1)
         ]
-        packet = jnp.concatenate([place] + listed + [jnp.zeros((4, rows), F32)], axis=0)
-        packet_out[oz + 1] = packet
-        if oz == 0:
+        packet = jnp.concatenate([place] + listed + [jnp.zeros((2, rows), F32)], axis=0)
+        packet_out[slot] = packet
+        if slot == 0:
             packet_in[0] = packet
     columns = jnp.concatenate([place, jnp.zeros((5, rows), F32)], axis=0).T
     for axis in range(3):
@@ -147,24 +144,14 @@
     started = []
 
     def spread(kind):
-        for ox, oz in beside:
-            src = packet_out.at[oz + 1] if kind == 0 else held_at(kind, 0)
+        for ox, oz in others:
+            src = packet_out.at[SLOT[ox, oz]] if kind == 0 else held_at(kind, 0)
             copy = send(kind, src, SLOT[-ox, -oz], ox, oz)
             copy.start()
             started.append(copy)
 
     def arrived(kind, slot):
         send(kind, held_at(kind, slot), slot, 1, 0).wait_recv()
-
-    def forward(kind, at):
-        arrived(kind, 3 + at)
-        for ox in (-1, 1):
-            copy = send(kind, held_at(kind, 3 + at), SLOT[-ox, -1] + at, ox, 0)
-            copy.start()
-            started.append(copy)
-
-    sooner = jnp.where(here[1] == 0, 1, 0)
-    later = 1 - sooner
 
     def build(ox, oz):
         slot = SLOT[ox, oz]
@@ -172,7 +159,7 @@
         other_x = packet[0:1] + 2.0 * ox
         other_y = packet[1:2]
         other_z = packet[2:3] + 2.0 * oz
-        middle_row = 7 - 3 * ox
+        middle_row = 4
         chunk = 32
         for c in range(2):
             cross = upper if c == 0 else jnp.logical_not(upper)
@@ -230,7 +217,7 @@
             total = term if total is None else total + term
         return total
 
-    pl.semaphore_wait(barrier, len(beside))
+    pl.semaphore_wait(barrier, len(others))
     spread(0)
     spread(1)
 
@@ -239,24 +226,10 @@
     build(0, 0)
     message = gathered(source, GROUPS[0], None)
     grad_act = nt(outw_ref[...], cot_ref[...])
-    forward(0, sooner)
-    forward(1, sooner)
-    for at in GROUPS[1]:
-        arrived(0, SLOT[at])
-        build(*at)
-    for at in GROUPS[1]:
-        arrived(1, SLOT[at])
-    message = gathered(source, GROUPS[1], message)
-    forward(0, later)
-    forward(1, later)
-    for at in GROUPS[2]:
-        build(*at)
-    message = gathered(source, GROUPS[2], message)
-    for group in GROUPS[3:]:
+    for group in GROUPS[1:]:
         for at in group:
             arrived(0, SLOT[at])
             build(*at)
-    for group in GROUPS[3:]:
         for at in group:
             arrived(1, SLOT[at])
         message = gathered(source, group, message)
@@ -269,19 +242,11 @@
 
     activated = (message * gate).astype(BF16)
     updated_ref[...] = (feat_ref[...].astype(F32) + tn(activated, outw_ref[...])).astype(BF16)
-    put_updated = pltpu.make_async_copy(updated_ref, updated_hbm, local_sem.at[8])
-    put_updated.start()
 
     total = gathered(grads, GROUPS[0], None)
-    forward(2, sooner)
-    for at in GROUPS[1]:
-        arrived(2, SLOT[at])
-    total = gathered(grads, GROUPS[1], total)
-    forward(2, later)
-    for group in GROUPS[2:]:
-        if group != GROUPS[2]:
-            for at in group:
-                arrived(2, SLOT[at])
+    for group in GROUPS[1:]:
+        for at in group:
+            arrived(2, SLOT[at])
         total = gathered(grads, group, total)
     at_row = lax.broadcasted_iota(jnp.int32, total.shape, 0)
     in_upper = at_row >= atoms
@@ -289,13 +254,9 @@
     grad_proj = jnp.where(kept, total, 0.0).astype(BF16)
     pulled = jnp.dot(grad_proj, proj_ref[...], preferred_element_type=F32)
     grad_ref[...] = (cot_ref[...].astype(F32) + pulled).astype(BF16)
-    put_grad = pltpu.make_async_copy(grad_ref, grad_hbm, local_sem.at[9])
-    put_grad.start()
 
     for copy in started:
         copy.wait_send()
-    put_updated.wait()
-    put_grad.wait()
 
 
 EXP_FALL = [2.718281828459045 ** (-4.0 * step) for step in range(8)]
@@ -322,15 +283,13 @@
     held = [pltpu.SMEM if at in (3, 4) else pltpu.VMEM for at in range(len(operands))]
     updated, grad = pl.pallas_call(
         functools.partial(kernel, atoms, bases),
-        out_shape=[jax.ShapeDtypeStruct((rows, channels), BF16)] * 2,
+        out_shape=[pltpu.VMEM((rows, channels), BF16)] * 2,
         in_specs=[pl.BlockSpec(memory_space=pl.ANY)] * len(operands),
-        out_specs=[pl.BlockSpec(memory_space=pl.ANY)] * 2,
+        out_specs=[pl.BlockSpec(memory_space=pltpu.VMEM)] * 2,
         scratch_shapes=[space(x.shape, x.dtype) for space, x in zip(held, operands)]
         + [
-            pltpu.VMEM((rows, channels), BF16),
-            pltpu.VMEM((rows, channels), BF16),
-            pltpu.VMEM((3, 16, rows), F32),
-            pltpu.VMEM((9, 16, rows), F32),
+            pltpu.VMEM((9, 8, rows), F32),
+            pltpu.VMEM((9, 8, rows), F32),
             pltpu.VMEM((3, rows, rows), F32),
             pltpu.VMEM((bases, rows, 9 * rows), BF16),
             pltpu.VMEM((width, 9 * rows), BF16),

time: 23.8 us -> 20.9 us (0.88)
  Pallas kernels: 20.9 us -> 18.8 us
  local copies, waits for them, and re-layouts: 2 us -> 1.23 us
    pallas_call x1, Pallas kernels: 20.9 us -> 18.8 us  [on_device(): pl.pallas_call(functools.partial(kernel, atoms, bases), out_shape=[pltpu....]
    unnamed x4 -> x2, local copies, waits for them, and re-layouts: 2 us -> 1.23 us
where the time goes in v3:
time: 20.9 us; the launch traced here: 20.7 us
  Pallas kernels  18.8 us (90%)
  local copies, waits for them, and re-layouts  1.23 us (6%)
  between operations  0.64 us (3%)
    pallas_call x1, Pallas kernels, on_device(): pl.pallas_call(functools.partial(kernel, atoms, bases), out_shape=[pltpu....  18.8 us
    unnamed x2, local copies, waits for them, and re-layouts  1.23 us

profile of v3, /device:TPU:0, one launch (start us, length us, event | category | flops | bytes accessed | tf_op | source)
XLA Modules:
  0.0 20.7 jit_solution(6401644558820175851)
XLA Ops:
  0.6 18.8 %shard_map.95 = (bf16[128,128]{1,0:T(8,128)(2,1)S(1)}, bf16[128,128]{1,0:T(8,128)(2,1)S(1)}) custom-call(bf16[128,128]{1,0:T(8,128)(2,1)} %bitcast.14, bf16[128,128]{1,0:T(8,128)(2,1)} %bitcast.15, f32[6,1,64]{2,1,0:T(1,128)} %bitcast.17, s32[2]{0:T(128)} %bitcast.19, s32[2,27]{1,0:T(2,128)} %bitcast.18, bf16[64,128]{1,0:T(8,128)(2,1)} %bitcast.16, ...), custom_call_target="tpu_custom_call" | custom-call | tf_op jit(solution)/shard_map/pallas_call | solution.py:284
  19.5 0.6 %copy.14 = bf16[1,2,1,64,128]{4,3,2,1,0:T(8,128)(2,1)} copy(bf16[1,2,1,64,128]{4,3,2,1,0:T(8,128)(2,1)S(1)} %bitcast.13) | data formatting | bytes 65536
  20.1 0.6 %copy.15 = bf16[1,2,1,64,128]{4,3,2,1,0:T(8,128)(2,1)} copy(bf16[1,2,1,64,128]{4,3,2,1,0:T(8,128)(2,1)S(1)} %bitcast.12) | data formatting | bytes 65536

commit v4 on v3

--- a/solution.py
+++ b/solution.py
@@ -9,7 +9,8 @@
 
 MESH = pl.DeviceIdType.MESH
 AXES = ("xy", "gz")
-GROUPS = (((0, 0),), ((-1, 0), (1, 0)), ((0, -1), (0, 1)), ((-1, -1), (-1, 1)), ((1, -1), (1, 1)))
+GROUPS = (((0, 0),), ((-1, 0), (1, 0)), ((0, -1), (-1, -1), (1, -1)), ((0, 1), (-1, 1), (1, 1)))
+ORDER = ((-1, None), (1, None), (-1, True), (1, True), (-1, False), (1, False), (0, True), (0, False))
 SLOT = {at: slot for slot, at in enumerate(at for group in GROUPS for at in group)}
 F32 = jnp.float32
 BF16 = jnp.bfloat16
@@ -38,8 +39,7 @@
     proj_hbm,
     outw_hbm,
     radial_hbm,
-    updated_ref,
-    grad_ref,
+    both_ref,
     feat_ref,
     cot_ref,
     pos_ref,
@@ -65,8 +65,10 @@
     def device_at(ox, oz):
         return (lax.rem(here[0] + ox + sizes[0], sizes[0]), lax.rem(here[1] + oz + sizes[1], sizes[1]))
 
+    sooner = jnp.where(here[1] == 0, 1, 0)
+    later = 1 - sooner
     barrier = pltpu.get_barrier_semaphore()
-    others = [at for at, slot in SLOT.items() if slot]
+    others = [(-1, 0), (1, 0), (-1, -1), (-1, 1), (1, -1), (1, 1), (0, -1), (0, 1)]
     for ox, oz in others[::-1]:
         pl.semaphore_signal(barrier, inc=1, device_id=device_at(ox, oz), device_id_type=MESH)
 
@@ -87,7 +89,7 @@
     ]
     for fetch in fetches:
         fetch.start()
-    for fetch in fetches[:5]:
+    for fetch in fetches[:3]:
         fetch.wait()
 
     lane = lax.broadcasted_iota(jnp.int32, (1, rows), 1)
@@ -119,13 +121,6 @@
         packet_out[slot] = packet
         if slot == 0:
             packet_in[0] = packet
-    columns = jnp.concatenate([place, jnp.zeros((5, rows), F32)], axis=0).T
-    for axis in range(3):
-        own_cols[axis] = jnp.broadcast_to(columns[:, axis : axis + 1], (rows, rows))
-
-    projected = nt(proj_ref[...], feat_ref[...])
-    source[:, lanes_of(0)] = (projected * valid_row).astype(BF16)
-
     def held_at(kind, slot):
         if kind == 0:
             return packet_in.at[slot]
@@ -144,21 +139,26 @@
     started = []
 
     def spread(kind):
-        for ox, oz in others:
-            src = packet_out.at[SLOT[ox, oz]] if kind == 0 else held_at(kind, 0)
-            copy = send(kind, src, SLOT[-ox, -oz], ox, oz)
+        for ox, side in ORDER:
+            if side is None:
+                mine, theirs, oz = SLOT[ox, 0], SLOT[-ox, 0], 0
+            else:
+                which = later if side else sooner
+                mine, theirs = SLOT[ox, -1] + 3 * which, SLOT[-ox, -1] + 3 * (1 - which)
+                oz = 2 * which - 1
+            src = packet_out.at[mine] if kind == 0 else held_at(kind, 0)
+            copy = send(kind, src, theirs, ox, oz)
             copy.start()
             started.append(copy)
 
     def arrived(kind, slot):
         send(kind, held_at(kind, slot), slot, 1, 0).wait_recv()
 
-    def build(ox, oz):
-        slot = SLOT[ox, oz]
+    def build(ox, oz, slot):
         packet = packet_in[slot]
         other_x = packet[0:1] + 2.0 * ox
         other_y = packet[1:2]
-        other_z = packet[2:3] + 2.0 * oz
+        other_z = packet[2:3] + (2.0 * oz if isinstance(oz, int) else 2.0 * oz.astype(F32))
         middle_row = 4
         chunk = 32
         for c in range(2):
@@ -185,7 +185,7 @@
                 near = jnp.minimum(dx * dx + dy * dy + dz * dz, 1.0)
                 room = 1.0 - near
                 envelope = room * room * gate
-                if slot == 0:
+                if isinstance(slot, int) and slot == 0:
                     at_row = lax.broadcasted_iota(jnp.int32, (chunk, rows), 0) + first
                     at_lane = lax.broadcasted_iota(jnp.int32, (chunk, rows), 1)
                     envelope = jnp.where(at_row == at_lane, 0.0, envelope)
@@ -207,9 +207,10 @@
 
             lax.fori_loop(0, atoms // chunk, part, 0)
 
-    def gathered(held, group, total):
-        width = len(group) * rows
-        span = pl.ds(SLOT[group[0]] * rows, width)
+    def gathered(held, slot, count, total):
+        width = count * rows
+        first = slot * rows
+        span = pl.ds(first if isinstance(slot, int) else pl.multiple_of(first, rows), width)
         stack = tiles[:, :, span].reshape(bases * rows, width)
         sums = nt(stack, held[:, span])
         for b in range(bases):
@@ -219,20 +220,34 @@
 
     pl.semaphore_wait(barrier, len(others))
     spread(0)
+    for fetch in fetches[3:5]:
+        fetch.wait()
+    projected = nt(proj_ref[...], feat_ref[...])
+    source[:, lanes_of(0)] = (projected * valid_row).astype(BF16)
     spread(1)
+    columns = jnp.concatenate([place, jnp.zeros((5, rows), F32)], axis=0).T
+    for axis in range(3):
+        own_cols[axis] = jnp.broadcast_to(columns[:, axis : axis + 1], (rows, rows))
+
 
     for fetch in fetches[5:]:
         fetch.wait()
-    build(0, 0)
-    message = gathered(source, GROUPS[0], None)
+    build(0, 0, 0)
+    message = gathered(source, 0, 1, None)
     grad_act = nt(outw_ref[...], cot_ref[...])
-    for group in GROUPS[1:]:
-        for at in group:
-            arrived(0, SLOT[at])
-            build(*at)
-        for at in group:
-            arrived(1, SLOT[at])
-        message = gathered(source, group, message)
+    for at in GROUPS[1]:
+        arrived(0, SLOT[at])
+        build(*at, SLOT[at])
+    for at in GROUPS[1]:
+        arrived(1, SLOT[at])
+    message = gathered(source, 1, 2, message)
+    for which, oz in ((sooner, 2 * sooner - 1), (later, 2 * later - 1)):
+        for at, ox in enumerate((0, -1, 1)):
+            arrived(0, 3 + 3 * which + at)
+            build(ox, oz, 3 + 3 * which + at)
+        for at in range(3):
+            arrived(1, 3 + 3 * which + at)
+        message = gathered(source, 3 + 3 * which, 3, message)
 
     message = message.T * valid_row
     gate = 1.0 / (1.0 + jnp.exp(-message))
@@ -241,19 +256,22 @@
     spread(2)
 
     activated = (message * gate).astype(BF16)
-    updated_ref[...] = (feat_ref[...].astype(F32) + tn(activated, outw_ref[...])).astype(BF16)
-
-    total = gathered(grads, GROUPS[0], None)
-    for group in GROUPS[1:]:
-        for at in group:
-            arrived(2, SLOT[at])
-        total = gathered(grads, group, total)
+    both_ref[0] = (feat_ref[...].astype(F32) + tn(activated, outw_ref[...])).astype(BF16)
+
+    total = gathered(grads, 0, 1, None)
+    for at in (1, 2):
+        arrived(2, at)
+    total = gathered(grads, 1, 2, total)
+    for which in (sooner, later):
+        for at in range(3):
+            arrived(2, 3 + 3 * which + at)
+        total = gathered(grads, 3 + 3 * which, 3, total)
     at_row = lax.broadcasted_iota(jnp.int32, total.shape, 0)
     in_upper = at_row >= atoms
     kept = (at_row - jnp.where(in_upper, atoms, 0)) < jnp.where(in_upper, counts_ref[1], counts_ref[0])
     grad_proj = jnp.where(kept, total, 0.0).astype(BF16)
     pulled = jnp.dot(grad_proj, proj_ref[...], preferred_element_type=F32)
-    grad_ref[...] = (cot_ref[...].astype(F32) + pulled).astype(BF16)
+    both_ref[1] = (cot_ref[...].astype(F32) + pulled).astype(BF16)
 
     for copy in started:
         copy.wait_send()
@@ -281,11 +299,11 @@
         radial_weight,
     )
     held = [pltpu.SMEM if at in (3, 4) else pltpu.VMEM for at in range(len(operands))]
-    updated, grad = pl.pallas_call(
+    both = pl.pallas_call(
         functools.partial(kernel, atoms, bases),
-        out_shape=[pltpu.VMEM((rows, channels), BF16)] * 2,
+        out_shape=pltpu.VMEM((2, rows, channels), BF16),
         in_specs=[pl.BlockSpec(memory_space=pl.ANY)] * len(operands),
-        out_specs=[pl.BlockSpec(memory_space=pltpu.VMEM)] * 2,
+        out_specs=pl.BlockSpec(memory_space=pltpu.VMEM),
         scratch_shapes=[space(x.shape, x.dtype) for space, x in zip(held, operands)]
         + [
             pltpu.VMEM((9, 8, rows), F32),
@@ -300,7 +318,7 @@
         ],
         compiler_params=pltpu.CompilerParams(collective_id=0, has_side_effects=True),
     )(*operands)
-    return updated.reshape(shape), grad.reshape(shape)
+    return both[0].reshape(shape), both[1].reshape(shape)
 
 
 def solution(mesh):

time: 20.9 us -> 18.8 us (0.90)
  Pallas kernels: 18.8 us -> 17.4 us
  local copies, waits for them, and re-layouts: 1.23 us -> 0.63 us
    pallas_call x1, Pallas kernels: 18.8 us -> 17.4 us  [on_device(): pl.pallas_call(functools.partial(kernel, atoms, bases), out_shape=pltpu.V...]
    unnamed x2 -> x0, local copies, waits for them, and re-layouts: 1.23 us -> none
    slice x0 -> x1, local copies, waits for them, and re-layouts: none -> 0.63 us  [on_device(): return (both[0].reshape(shape), both[1].reshape(shape))]
where the time goes in v4:
time: 18.8 us; the launch traced here: 18.7 us
  Pallas kernels  17.4 us (93%)
  between operations  0.64 us (3%)
  local copies, waits for them, and re-layouts  0.63 us (3%)
    pallas_call x1, Pallas kernels, on_device(): pl.pallas_call(functools.partial(kernel, atoms, bases), out_shape=pltpu.V...  17.4 us
    slice x1, local copies, waits for them, and re-layouts, on_device(): return (both[0].reshape(shape), both[1].reshape(shape))  0.63 us

profile of v4, /device:TPU:0, one launch (start us, length us, event | category | flops | bytes accessed | tf_op | source)
XLA Modules:
  0.0 18.7 jit_solution(9705127746524109847)
XLA Ops:
  0.6 17.4 %shard_map.95 = bf16[2,128,128]{2,1,0:T(8,128)(2,1)S(1)} custom-call(bf16[128,128]{1,0:T(8,128)(2,1)} %bitcast.12, bf16[128,128]{1,0:T(8,128)(2,1)} %bitcast.13, f32[6,1,64]{2,1,0:T(1,128)} %bitcast.17, s32[2]{0:T(128)} %bitcast.19, s32[2,27]{1,0:T(2,128)} %bitcast.18, bf16[64,128]{1,0:T(8,128)(2,1)} %bitcast.16, bf16[64,128]{1,0:T(8,128)(2,1)} %outw_hbm.1, ...), custom_call_target="tpu_custom_call" | custom-call | tf_op jit(solution)/shard_map/pallas_call | solution.py:302
  18.0 0.6 %fusion = (bf16[1,128,128]{2,1,0:T(8,128)(2,1)}, bf16[1,128,128]{2,1,0:T(8,128)(2,1)}) fusion(bf16[2,128,128]{2,1,0:T(8,128)(2,1)S(1)} %shard_map.95), kind=kLoop, calls=%fused_computation | loop fusion | bytes 131072 | tf_op jit(solution)/shard_map/slice | solution.py:321
